TPU v7x, 128 devices: a whole 4x4x4 slice. The times are simulated.
128 devices in a mesh: energy: 32 (over z, y, core), space: 4 (over x).
Axes of the slice: x: 4, y: 4, z: 4, core: 2. Of those that a mesh axis runs over, the one named last changes fastest.
Arguments:
- ham_diag: float32 [4, 256, 256], P('space')
- ham_coup: float32 [4, 256, 256], P('space'), may hold values from -0.1875 to 0.1875
- energies: float32 [32], P('energy'), may hold values from 1 to 2
- pattern: int32 [4, 43264], P('space'), may hold values from 0 to 65535, as said below
- coulomb: float32 [4, 43264], P('space', 'energy'), may hold values from 0.5 to 2
Outputs:
- green: float32 [32, 4, 256, 256], P('energy', 'space')
- screened: float32 [32, 4, 43264], P(None, 'space', 'energy')
Inputs may be any that keep to these rules, and one draw needn't show every extreme that they name: `pattern`: each row holds 43264 distinct flat positions of one block, among them all 256 diagonal positions.
All inputs are finite; a program needn't handle non-finite values.
Results may differ from a plain program's by a relative error of at most 0.0001.
Values sent between devices are 32-bit elements; how exact they have to be, the bound alone decides.
A program may use at most 128 MiB of HBM per device.

v0:
```python
import functools

import jax
import jax.numpy as jnp
from jax import lax
from jax.experimental import pallas as pl
from jax.experimental.pallas import tpu as pltpu
from jax.sharding import PartitionSpec as P

F32, BF16 = jnp.float32, jnp.bfloat16
MESH = pl.DeviceIdType.MESH
VMEM = pltpu.VMEM
DMA = pltpu.SemaphoreType.DMA

polar_coef = 128.0
sigma_coef = 0.5

TOLERANCE = 2e-5
VMEM_LIMIT = 20 << 20


def split(value):
    high = value.astype(BF16)
    return high, (value - high.astype(F32)).astype(BF16)


def dot(a, b):
    return jnp.dot(a, b, preferred_element_type=F32)


def dot_nt(a, b):
    return lax.dot_general(a, b, (((1,), (1,)), ((), ())), preferred_element_type=F32)


def mul(a, b):
    return dot(a[0], b[0]) + (dot(a[0], b[1]) + dot(a[1], b[0]))


def product(a, b):
    return mul(split(a), split(b))


def identity(width):
    rows = lax.broadcasted_iota(jnp.int32, (width, width), 0)
    cols = lax.broadcasted_iota(jnp.int32, (width, width), 1)
    return jnp.where(rows == cols, 1.0, 0.0).astype(F32)


def series(matrices, scales, doublings):
    ident = identity(matrices[0].shape[0])
    parts = [split(matrix) for matrix in matrices]
    squares = [mul(own, own) for own in parts]
    powers = [
        ident - matrix * (2.0 * scale) + square * (scale * scale)
        for matrix, scale, square in zip(matrices, scales, squares)
    ]
    guesses = [scale * (2.0 * ident - matrix * scale) for matrix, scale in zip(matrices, scales)]
    guesses = [guess + product(guess, power) for guess, power in zip(guesses, powers)]
    for _ in range(doublings - 1):
        highs = [power.astype(BF16) for power in powers]
        powers = [dot(high, high) for high in highs]
        guesses = [
            guess + dot(guess.astype(BF16), power.astype(BF16)) for guess, power in zip(guesses, powers)
        ]
    return guesses


def total_of(value):
    return jnp.sum(jnp.sum(value, axis=0, keepdims=True), axis=1, keepdims=True)


def mean_scale(matrix):
    trace = total_of(jnp.where(identity(matrix.shape[0]) > 0.0, matrix, 0.0))
    return trace / total_of(matrix * matrix)


def safe_scale(matrix):
    return 1.9 / jnp.max(jnp.sum(jnp.abs(matrix), axis=0, keepdims=True), axis=1, keepdims=True)


def eliminate(matrix, out_ref):
    width = matrix.shape[0]
    out_ref[...] = matrix
    lanes = lax.broadcasted_iota(jnp.int32, (1, width), 1)

    def step(pivot, carry):
        whole = out_ref[...]
        row = out_ref[pl.ds(pivot, 1), :]
        here = lanes == pivot
        value = jnp.sum(jnp.where(here, row, 0.0), axis=1, keepdims=True)
        column = jnp.sum(jnp.where(here, whole, 0.0), axis=1, keepdims=True)
        scaled = jnp.where(here, 1.0, row) / value
        out_ref[...] = jnp.where(here, 0.0, whole) - column * scaled
        out_ref[pl.ds(pivot, 1), :] = scaled
        return carry

    lax.fori_loop(0, width, step, 0)


def newton_step(parts, guesses):
    ident = identity(guesses[0].shape[0])
    split_guesses = [split(guess) for guess in guesses]
    residuals = [ident - mul(own, guess) for own, guess in zip(parts, split_guesses)]
    better = [
        guess + dot(guess_parts[0], residual.astype(BF16))
        for guess, guess_parts, residual in zip(guesses, split_guesses, residuals)
    ]
    return better, [residual * residual for residual in residuals]


def newton(matrices, refs, limit, worst=1.0):
    parts = [split(matrix) for matrix in matrices]

    def unsettled(carry):
        steps, last = carry
        return jnp.logical_and(last > TOLERANCE, steps < limit)

    def step(carry):
        better, squares = newton_step(parts, [ref[...] for ref in refs])
        largest = jnp.float32(0.0)
        for ref, value, square in zip(refs, better, squares):
            ref[...] = value
            largest = jnp.maximum(largest, jnp.sum(square))
        return carry[0] + 1, largest

    return lax.while_loop(unsettled, step, (jnp.int32(0), jnp.asarray(worst, F32)))[1]


def settle(matrices, refs, worst=1.0):
    worst = newton(matrices, refs, 8, worst)

    @pl.when(jnp.logical_not(worst <= TOLERANCE))
    def _():
        for matrix, ref in zip(matrices, refs):
            ref[...] = series([matrix], [safe_scale(matrix)], 5)[0]
        again = newton(matrices, refs, 48)

        @pl.when(jnp.logical_not(again <= TOLERANCE))
        def _():
            for matrix, ref in zip(matrices, refs):
                eliminate(matrix, ref)


def quick(matrices):
    guesses = series(matrices, [mean_scale(matrix) for matrix in matrices], 3)
    return newton_step([split(matrix) for matrix in matrices], guesses)


def peer_of(me, offset):
    core = lax.rem(me + offset, 2)
    y = lax.rem(me // 2 + offset // 2, 4)
    z = lax.rem(me // 8 + offset // 8, 4)
    return z * 8 + y * 2 + core


def peers_of(count, me):
    cores = [lax.rem(me + step, 2) for step in range(2)]
    ys = [lax.rem(me // 2 + step, 4) * 2 for step in range(4)]
    zs = [lax.rem(me // 8 + step, 4) * 8 for step in range(4)]
    return [zs[offset // 8] + ys[offset // 2 % 4] + cores[offset % 2] for offset in range(count - 1, 0, -1)]


def to_peer(peer, source, target, sems):
    return pltpu.make_async_remote_copy(
        src_ref=source, dst_ref=target, send_sem=sems.at[0], recv_sem=sems.at[1],
        device_id={"energy": peer}, device_id_type=MESH,
    )


def rows_of(ref, peer):
    return ref.at[pl.ds(pl.multiple_of(peer * 8, 8), 8), :]


def collect_kernel(
    count, spaces, diag_ref, coup_ref, pattern_ref, bare_ref,
    diags_ref, coups_ref, rows_ref, slots_ref, bare_pos_ref, bare_own_ref,
    pattern, bare_in, own_pattern, own_bare, scattered, from_core, by_y, from_y, by_z, from_z,
    own_sem, far_send, far_recv, near_send, near_recv, more_sems, core_sems, y_send, y_recv, z_send, z_recv,
):
    me = lax.axis_index("energy")
    place = lax.axis_index("space")
    width = diag_ref.shape[1]
    half = width // 2
    core = lax.rem(me, 2)
    other = me + 1 - 2 * core
    own_y = lax.rem(me // 2, 4)
    own_z = me // 8
    span = bare_ref.shape[1]
    chunk = own_bare.shape[1]
    sides = (lax.rem(place + 1, spaces), lax.rem(place + spaces - 1, spaces))
    across = lax.rem(place + 2, spaces)

    own_copies = [
        pltpu.make_async_copy(pattern_ref, pattern, own_sem.at[0]),
        pltpu.make_async_copy(bare_ref, bare_in, own_sem.at[1]),
        pltpu.make_async_copy(diag_ref.at[0], diags_ref.at[place], own_sem.at[2]),
        pltpu.make_async_copy(coup_ref.at[0], coups_ref.at[place], own_sem.at[3]),
    ]
    for copy in own_copies:
        copy.start()

    barrier = pltpu.get_barrier_semaphore()
    for side in sides:
        pl.semaphore_signal(barrier, inc=1, device_id={"space": side}, device_id_type=MESH)
    for step in (2, 1, 3):
        for stride in (2, 8):
            pl.semaphore_signal(
                barrier, inc=1, device_id={"energy": peer_of(me, step * stride)}, device_id_type=MESH)
    pl.semaphore_signal(barrier, inc=1, device_id={"energy": other}, device_id_type=MESH)

    own_copies[0].wait()
    own_copies[1].wait()
    tail = chunk - 128
    for part in range(count):
        size = chunk if part < count - 1 else span
        if size < chunk:
            own_pattern[part, :, tail:] = jnp.zeros((1, 128), jnp.int32)
            rows_ref[part, :, tail:] = jnp.zeros((1, 128), jnp.int32)
            slots_ref[part, :, tail:] = jnp.zeros((1, 128), jnp.int32)
        piece = pattern[:, part * span:part * span + size]
        own_pattern[part, :, :size] = piece
        row = lax.shift_right_logical(piece, 8)
        col = jnp.bitwise_and(piece, 255)
        high = jnp.maximum(row, col)
        low = jnp.minimum(row, col)
        lower = low >= 128
        pivot = high == low
        rows_ref[part, :, :size] = jnp.where(jnp.logical_and(lower, jnp.logical_not(pivot)), low - 128, high)
        slots_ref[part, :, :size] = jnp.where(lower, jnp.where(pivot, 128, high - 128), low)
    own_bare[:, tail:] = jnp.zeros((1, 128), F32)
    own_bare[:, :span] = bare_in[...]

    pl.semaphore_wait(barrier, 9)
    own_half = pl.ds(pl.multiple_of(core * half, half), half)
    other_half = pl.ds(pl.multiple_of((1 - core) * half, half), half)
    given = (diag_ref, coup_ref)
    stores = (diags_ref, coups_ref)

    own_quarter = pl.ds(pl.multiple_of(half + core * (half // 2), half // 2), half // 2)
    other_quarter = pl.ds(pl.multiple_of(half + (1 - core) * (half // 2), half // 2), half // 2)

    class Pieces:
        def __init__(self, kind, source, store, part, quarter, sems, device):
            views = ((part,),) if kind else ((part, part), (quarter, pl.ds(0, half)))
            self.copies = [
                pltpu.make_async_remote_copy(
                    src_ref=source.at[view], dst_ref=store.at[view], send_sem=sems[0][at], recv_sem=sems[1][at],
                    device_id=device, device_id_type=MESH)
                for at, view in enumerate(views)
            ]

        def start(self):
            for copy in self.copies:
                copy.start()

        def wait_send(self):
            for copy in self.copies:
                copy.wait_send()

        def wait_recv(self):
            for copy in self.copies:
                copy.wait_recv()

    def far(way, stage):
        kind = (way, 1 - way, way)[stage]
        block = place if stage < 2 else sides[1 - way]
        store = stores[kind].at[block]
        source = given[kind].at[0] if stage < 2 else store
        sems = (
            (far_send.at[way, stage], more_sems.at[way, stage, 0]),
            (far_recv.at[way, stage], more_sems.at[way, stage, 1]),
        )
        return Pieces(kind, source, store, own_half, own_quarter, sems, {"space": sides[way]})

    def near(way, stage, own):
        kind = (way, 1 - way, way)[stage]
        block = sides[1 - way] if stage < 2 else across
        store = stores[kind].at[block]
        sems = (
            (near_send.at[way, stage], more_sems.at[way, stage, 2]),
            (near_recv.at[way, stage], more_sems.at[way, stage, 3]),
        )
        part, quarter = (own_half, own_quarter) if own else (other_half, other_quarter)
        return Pieces(kind, store, store, part, quarter, sems, {"energy": other})

    for stage in range(2):
        for way in range(2):
            far(way, stage).start()

    mine = own_pattern[me]
    bare = own_bare[...]
    index = lax.broadcasted_iota(jnp.int32, (width, chunk), 0)
    on_row = index == lax.shift_right_logical(mine, 8)
    on_col = jnp.where(index == jnp.bitwise_and(mine, 255), 1.0, 0.0).astype(BF16)
    rest = bare
    total = None
    for _ in range(3):
        part = rest.astype(BF16).astype(F32)
        rest = rest - part
        term = dot_nt(jnp.where(on_row, part, 0.0).astype(BF16), on_col)
        total = term if total is None else total + term
    for peer in range(count):
        scattered[peer % 2, peer // 2 % 4, peer // 8] = total[peer * 8:peer * 8 + 8, :]
    for line in range(chunk // 128):
        bare_own_ref[line:line + 1, :] = bare[:, line * 128:(line + 1) * 128]
    for line in range(chunk // 128, bare_own_ref.shape[0]):
        bare_own_ref[line:line + 1, :] = jnp.zeros((1, 128), F32)

    to_core = pltpu.make_async_remote_copy(
        src_ref=scattered.at[1 - core], dst_ref=from_core,
        send_sem=core_sems.at[0], recv_sem=core_sems.at[1],
        device_id={"energy": other}, device_id_type=MESH)

    def to_y(step):
        return pltpu.make_async_remote_copy(
            src_ref=by_y.at[lax.rem(own_y + step, 4)], dst_ref=from_y.at[step],
            send_sem=y_send.at[step], recv_sem=y_recv.at[step],
            device_id={"energy": peer_of(me, 2 * step)}, device_id_type=MESH)

    def to_z(step):
        return pltpu.make_async_remote_copy(
            src_ref=by_z.at[lax.rem(own_z + step, 4)], dst_ref=from_z.at[step],
            send_sem=z_send.at[step], recv_sem=z_recv.at[step],
            device_id={"energy": peer_of(me, 8 * step)}, device_id_type=MESH)

    to_core.start()
    for way in range(2):
        far(way, 0).wait_recv()
        far(way, 2).start()
        near(way, 0, True).start()
    to_core.wait()
    for y in range(4):
        for z in range(4):
            by_y[y, z] = scattered[core, y, z] + from_core[y, z]
    for step in (2, 1, 3):
        to_y(step).start()
    for step in (1, 3, 2):
        to_y(step).wait()
    for z in range(4):
        by_z[z] = (by_y[own_y, z] + from_y[1, z]) + (from_y[2, z] + from_y[3, z])
    for step in (2, 1, 3):
        to_z(step).start()
    for stage in (1, 2):
        for way in range(2):
            far(way, stage).wait_recv()
            near(way, stage, True).start()
    for step in (1, 3, 2):
        to_z(step).wait()
    bare_pos_ref[...] = (by_z[own_z] + from_z[1]) + (from_z[2] + from_z[3])
    for copy in own_copies[2:]:
        copy.wait()
    for stage in range(3):
        for way in range(2):
            far(way, stage).wait_send()
            near(way, stage, True).wait_send()
            near(way, stage, False).wait_recv()


def chain_kernel(
    shift_ref, diags_ref, coups_ref, reduced_ref, base_ref,
    v_ref, vt_ref, w_ref, wt_ref, c_ref, ct_ref, last_ref, x_ref, y_ref,
):
    place = lax.axis_index("space")
    width = base_ref.shape[0]
    lead_parts = split(coups_ref[3])
    quarter = (
        dot_nt(lead_parts[0], lead_parts[0])
        + (dot_nt(lead_parts[0], lead_parts[1]) + dot_nt(lead_parts[1], lead_parts[0]))
    ) * 0.25

    def whole(block):
        half = width // 2
        left = diags_ref[block, :, :half]
        right = diags_ref[block, half:, half:]
        return jnp.concatenate([left, jnp.concatenate([left[half:].T, right], axis=0)], axis=1)

    last_ref[...] = whole(3) - quarter
    lower = place <= 1
    at_end = jnp.logical_or(place == 0, place == 3)

    def choose(block, flipped, ref, turned_ref):
        value = coups_ref[block]
        turned = value.T
        ref[...] = jnp.where(flipped, turned, value)
        turned_ref[...] = jnp.where(flipped, value, turned)

    first = jnp.where(place == 0, 1, jnp.where(place == 1, 0, jnp.where(place == 2, 3, 2)))
    second = jnp.where(lower, 3, 0)
    middle = jnp.where(lower, 2, 1)
    choose(1, jnp.logical_not(lower), c_ref, ct_ref)
    choose(jnp.where(lower, 2, 0), lower, v_ref, vt_ref)
    choose(jnp.where(lower, 0, 2), lax.rem(place, 2) == 0, w_ref, wt_ref)
    shift = identity(width) * shift_ref[0]

    def system(block):
        return jnp.where(block == 3, last_ref[...], whole(block)) + shift

    def run(solve):
        x, y = solve([system(first), system(second)], [x_ref, y_ref])
        x, y = split(x), split(y)
        wt_s, ut_s = split(wt_ref[...]), split(ct_ref[...])
        xw = split(mul(x, split(w_ref[...])))
        yv = split(mul(y, split(v_ref[...])))
        xu = split(mul(x, split(c_ref[...])))
        rest = system(place) - mul(wt_s, xw)
        inner = system(middle) - mul(split(vt_ref[...]), yv) - jnp.where(at_end, mul(ut_s, xu), 0.0)
        c = jnp.where(at_end, mul(wt_s, xu), c_ref[...])
        ct = jnp.where(at_end, mul(ut_s, xw), ct_ref[...])
        (z,) = solve([inner], [x_ref])
        reduced = rest - mul(split(product(c, z)), split(ct))
        reduced_ref[...] = reduced
        (base,) = solve([reduced], [base_ref])
        return base

    squares = []

    def solve_quickly(matrices, refs):
        inverses, residuals = quick(matrices)
        squares.extend(residuals)
        return inverses

    base_ref[...] = run(solve_quickly)
    worst = total_of(squares[0])
    for square in squares[1:]:
        worst = jnp.maximum(worst, total_of(square))
    worst = jnp.where(worst <= TOLERANCE, worst, 2.0 * TOLERANCE)

    @pl.when(jnp.logical_not(jnp.max(worst) <= TOLERANCE))
    def _():
        def solve_surely(matrices, refs):
            for matrix, ref in zip(matrices, refs):
                ref[...] = series([matrix], [mean_scale(matrix)], 3)[0]
            settle(matrices, refs)
            return [ref[...] for ref in refs]

        base_ref[...] = run(solve_surely)


def screen(samples, bare, scale):
    count = len(samples)
    result = []
    for lag in range(count):
        total = samples[0] * samples[lag]
        for m in range(1, count - lag):
            total = total + samples[m] * samples[m + lag]
        scaled = bare * (total * scale)
        result.append(bare * lax.rsqrt(1.0 + scaled * scaled))
    return result


PAIRS_FIRST = 2
PAIRS_SECOND = 9


def regroup_kernel(
    count, base_ref, rows_ref, slots_ref, bare_pos_ref, spread_ref, taken_ref,
    lhs, arrived, selfen, taken, sems_a, sems_b, sems_c,
):
    me = lax.axis_index("energy")
    width = base_ref.shape[0]
    half = width // 2
    chunk = rows_ref.shape[2]
    lines = taken.shape[1]
    pairs = count // 2
    for peer in range(count):
        taken_ref[peer, chunk // 128:, :] = jnp.zeros((lines - chunk // 128, 128), F32)

    barrier = pltpu.get_barrier_semaphore()

    others = peers_of(count, me)
    for peer in others:
        pl.semaphore_signal(barrier, inc=1, device_id={"energy": peer}, device_id_type=MESH)
    arrived[me] = rows_of(base_ref, me)[...]

    upper = base_ref[:half, :half]
    lower = base_ref[half:, half:]
    r = lax.broadcasted_iota(jnp.int32, (half, half), 0)
    c = lax.broadcasted_iota(jnp.int32, (half, half), 1)
    table = jnp.concatenate([jnp.where(r <= c, upper, lower), base_ref[:half, half:]], axis=1)
    diagonal = jnp.sum(jnp.where(r == c, lower, 0.0), axis=0, keepdims=True)
    extra = jnp.concatenate([jnp.zeros((1, half), F32), diagonal], axis=1)
    first = lax.broadcasted_iota(jnp.int32, (8, width), 0) == 0
    table = jnp.concatenate([table, jnp.where(first, extra, 0.0)], axis=0)
    tall = table.shape[0]
    high = table.astype(BF16).astype(F32)
    lhs[...] = jnp.concatenate([high, table - high], axis=0).astype(BF16)
    row_index = lax.broadcasted_iota(jnp.int32, (width, chunk), 0).astype(F32).astype(BF16)
    line_index = lax.broadcasted_iota(jnp.int32, (8, chunk), 0)
    one, none = jnp.bfloat16(1), jnp.bfloat16(0)

    def take(part):
        hot = jnp.where(row_index == rows_ref[part].astype(F32).astype(BF16), one, none)
        both = dot(lhs[...], hot)
        slots = slots_ref[part]
        group = jnp.broadcast_to(lax.shift_right_logical(slots, 3), (8, chunk))
        found, found_rest = both[:8], both[tall:tall + 8]
        for at in range(1, tall // 8):
            here = group == at
            found = jnp.where(here, both[at * 8:at * 8 + 8], found)
            found_rest = jnp.where(here, both[tall + at * 8:tall + at * 8 + 8], found_rest)
        here = line_index == jnp.bitwise_and(slots, 7)
        line = jnp.sum(jnp.where(here, found + found_rest, 0.0), axis=0, keepdims=True)
        for piece in range(chunk // 128):
            taken[part, piece:piece + 1, :] = line[:, piece * 128:(piece + 1) * 128]

    filled = chunk // 128

    def all_but_one(source, target, sems):
        return to_peer(others[0], source, target, sems)

    def take_pair(pair, carry):
        take(peer_of(me, count - 1 - 2 * pair))
        take(peer_of(me, count - 2 - 2 * pair))
        return carry

    def send_taken(peer):
        to_peer(peer, taken.at[peer, :filled], taken_ref.at[me, :filled], sems_c).start()

    def send_pair(pair, carry):
        for offset in (count - 1 - 2 * pair, count - 2 - 2 * pair):
            send_taken(peer_of(me, offset))
        return carry

    def take_and_send(pair, carry):
        take_pair(pair, carry)
        return send_pair(pair, carry)

    lax.fori_loop(0, PAIRS_FIRST, take_pair, 0)
    pl.semaphore_wait(barrier, count - 1)
    for peer in others:
        to_peer(peer, rows_of(base_ref, peer), arrived.at[me], sems_a).start()
    lax.fori_loop(0, PAIRS_FIRST, send_pair, 0)
    lax.fori_loop(PAIRS_FIRST, PAIRS_FIRST + PAIRS_SECOND, take_and_send, 0)
    rest = pl.ds(8, width - 8)
    first_exchange = all_but_one(base_ref.at[rest, :], arrived.at[pl.ds(1, count - 1)], sems_a)
    first_exchange.wait_send()
    first_exchange.wait_recv()

    scale = polar_coef * width / count
    for side in range(width // 128):
        cols = slice(side * 128, (side + 1) * 128)
        samples = [arrived[e, :, cols] for e in range(count)]
        screened = screen(samples, bare_pos_ref[:, cols], scale)
        for e in range(count):
            total = samples[e] * screened[0]
            for n in range(1, e + 1):
                total = total + samples[e - n] * screened[n]
            selfen[e, :, cols] = total * (sigma_coef / count)
    for peer in others:
        to_peer(peer, selfen.at[peer], rows_of(spread_ref, me), sems_b).start()
    lax.fori_loop(PAIRS_FIRST + PAIRS_SECOND, pairs - 1, take_and_send, 0)
    take_pair(pairs - 1, 0)
    send_taken(peer_of(me, 1))
    taken_ref[me, :filled] = taken[me, :filled]
    spread_ref[pl.ds(pl.multiple_of(me * 8, 8), 8), :] = selfen[me]
    for last_exchange in (
        all_but_one(selfen.at[pl.ds(1, count - 1)], spread_ref.at[rest, :], sems_b),
        all_but_one(taken.at[pl.ds(1, count - 1), :filled], taken_ref.at[pl.ds(1, count - 1), :filled], sems_c),
    ):
        last_exchange.wait_send()
        last_exchange.wait_recv()


def finish_kernel(reduced_ref, base_ref, spread_ref, taken_ref, bare_ref, green_ref, screened_ref, x_ref):
    count = taken_ref.shape[0]
    width = base_ref.shape[0]
    chunk = screened_ref.shape[2]
    spread = spread_ref[...]
    matrix = reduced_ref[...] - 0.5 * (spread + spread.T)
    parts = split(matrix)
    base = base_ref[...]
    base_parts = split(base)
    residual = identity(width) - mul(parts, base_parts)
    near = residual.astype(BF16)
    guess = base + dot(base_parts[0], (residual + dot(near, near)).astype(BF16))
    (better,), (square,) = newton_step([parts], [guess])
    x_ref[...] = better

    scale = polar_coef * width / count
    for group in range(taken_ref.shape[1] // 8):
        at = slice(group * 8, group * 8 + 8)
        samples = [taken_ref[e, at, :] for e in range(count)]
        screened = screen(samples, bare_ref[at, :], scale)
        for line in range(group * 8, min(group * 8 + 8, pl.cdiv(chunk, 128))):
            start = line * 128
            stop = min(start + 128, chunk)
            for n in range(count):
                row = line - group * 8
                screened_ref[n, :, start:stop] = screened[n][row:row + 1, :stop - start]

    settle([matrix], [x_ref], jnp.sum(square))
    green_ref[0, 0] = x_ref[...]


def on_device(count, spaces, ham_diag, ham_coup, energies, pattern, coulomb):
    width = ham_diag.shape[1]
    span = coulomb.shape[1]
    chunk = pl.cdiv(span, 128) * 128
    lines = pl.cdiv(chunk // 128, 8) * 8
    vmem = pl.BlockSpec(memory_space=pltpu.VMEM)
    hbm = pl.BlockSpec(memory_space=pltpu.HBM)
    smem = pl.BlockSpec(memory_space=pltpu.SMEM)
    square = jax.ShapeDtypeStruct((width, width), F32)
    diags, coups, rows, slots, bare_pos, bare_own = pl.pallas_call(
        functools.partial(collect_kernel, count, spaces),
        out_shape=(
            jax.ShapeDtypeStruct((spaces, width, width), F32),
            jax.ShapeDtypeStruct((spaces, width, width), F32),
            jax.ShapeDtypeStruct((count, 1, chunk), jnp.int32),
            jax.ShapeDtypeStruct((count, 1, chunk), jnp.int32),
            jax.ShapeDtypeStruct((8, width), F32),
            jax.ShapeDtypeStruct((lines, 128), F32),
        ),
        in_specs=[hbm] * 4,
        out_specs=(vmem,) * 6,
        scratch_shapes=[
            VMEM((1, pattern.shape[1]), jnp.int32), VMEM((1, span), F32),
            VMEM((count, 1, chunk), jnp.int32), VMEM((1, chunk), F32),
            VMEM((2, 4, 4, 8, width), F32), VMEM((4, 4, 8, width), F32), VMEM((4, 4, 8, width), F32),
            VMEM((4, 4, 8, width), F32), VMEM((4, 8, width), F32), VMEM((4, 8, width), F32),
            DMA((4,)), DMA((2, 3)), DMA((2, 3)), DMA((2, 3)), DMA((2, 3)), DMA((2, 3, 4)),
            DMA((2,)), DMA((4,)), DMA((4,)), DMA((4,)), DMA((4,)),
        ],
        compiler_params=pltpu.CompilerParams(collective_id=0, has_side_effects=True, vmem_limit_bytes=VMEM_LIMIT),
        name="collect",
    )(*(pltpu.with_memory_space_constraint(value, pltpu.HBM) for value in (
        ham_diag, ham_coup, pattern, coulomb)))

    reduced, base = pl.pallas_call(
        chain_kernel,
        out_shape=(square, square),
        in_specs=[smem, vmem, vmem],
        out_specs=(vmem, vmem),
        scratch_shapes=[VMEM((width, width), F32)] * 9,
        compiler_params=pltpu.CompilerParams(vmem_limit_bytes=VMEM_LIMIT),
        name="chain",
    )(energies, diags, coups)

    spread, taken = pl.pallas_call(
        functools.partial(regroup_kernel, count),
        out_shape=(square, jax.ShapeDtypeStruct((count, lines, 128), F32)),
        in_specs=[vmem] * 4,
        out_specs=(vmem, vmem),
        scratch_shapes=[
            VMEM((width + 16, width), BF16), VMEM((count, 8, width), F32),
            VMEM((count, 8, width), F32), VMEM((count, lines, 128), F32),
        ] + [DMA((2,))] * 3,
        compiler_params=pltpu.CompilerParams(collective_id=1, has_side_effects=True, vmem_limit_bytes=VMEM_LIMIT),
        name="regroup",
    )(base, rows, slots, bare_pos)

    return pl.pallas_call(
        finish_kernel,
        out_shape=(
            jax.ShapeDtypeStruct((1, 1, width, width), F32),
            jax.ShapeDtypeStruct((count, 1, span), F32),
        ),
        in_specs=[vmem] * 5,
        out_specs=(vmem, vmem),
        scratch_shapes=[VMEM((width, width), F32)],
        compiler_params=pltpu.CompilerParams(vmem_limit_bytes=VMEM_LIMIT),
        name="finish",
    )(reduced, base, spread, taken, bare_own)


def solution(mesh):
    count, spaces = mesh.shape["energy"], mesh.shape["space"]
    return jax.shard_map(
        functools.partial(on_device, count, spaces),
        mesh=mesh,
        in_specs=(
            P("space", None, None),
            P("space", None, None),
            P("energy"),
            P("space", None),
            P("space", "energy"),
        ),
        out_specs=(P("energy", "space", None, None), P(None, "space", "energy")),
        check_vma=False,
    )
```

profile of v0, /device:TPU:1, one launch (start us, length us, event | category | flops | bytes accessed | tf_op | source)
XLA Modules:
  0.0 47.8 jit_solution(4961911879103684144)
XLA Ops:
  1.3 19.6 %collect.1 = (f32[4,256,256]{2,1,0:T(8,128)S(1)}, f32[4,256,256]{2,1,0:T(8,128)S(1)}, s32[32,1,1408]{2,1,0:T(1,128)S(1)}, s32[32,1,1408]{2,1,0:T(1,128)S(1)}, f3...) custom-call(f32[1,256,256]{2,1,0:T(8,128)} %diag_ref.1, f32[1,256,256]{2,1,0:T(8,128)} %coup_ref.1, s32[1,43264]{1,0:T(1,128)} %pattern_ref.1, ...), custom_call_target="tpu_custom_call" | custom-call | tf_op jit(solution)/shard_map/collect/pallas_call | solution.py:604
  20.8 6.6 %chain.1 = (f32[256,256]{1,0:T(8,128)S(1)}, f32[256,256]{1,0:T(8,128)S(1)}) custom-call(f32[1]{0:T(128)S(6)} %copy.7.shift_ref, f32[4,256,256]{2,1,0:T(8,128)S(1)} %get-tuple-element.12.diags_ref, f32[4,256,256]{2,1,0:T(8,128)S(1)} %get-tuple-element.13.coups_ref), custom_call_target="tpu_custom_call" | custom-call | tf_op jit(solution)/shard_map/chain/pallas_call | solution.py:629
  27.4 17.9 %regroup.1 = (f32[256,256]{1,0:T(8,128)S(1)}, f32[32,16,128]{2,1,0:T(8,128)S(1)}) custom-call(f32[256,256]{1,0:T(8,128)S(1)} %get-tuple-element.15.base_ref, s32[32,1,1408]{2,1,0:T(1,128)S(1)} %get-tuple-element.16.rows_ref, s32[32,1,1408]{2,1,0:T(1,128)S(1)} %get-tuple-element.17.slots_ref, f32[8,256]{1,0:T(8,128)S(1)} %get-tuple-element.18.bare_pos_ref), custom_call_target="tpu_custom_call" | custom-call | tf_op jit(solution)/shard_map/regroup/pallas_call | solution.py:639
  45.4 2.4 %finish.1 = (f32[1,1,256,256]{3,2,1,0:T(8,128)}, f32[32,1,1352]{2,1,0:T(1,128)}) custom-call(f32[256,256]{1,0:T(8,128)S(1)} %get-tuple-element.14.reduced_ref, f32[256,256]{1,0:T(8,128)S(1)} %get-tuple-element.15.base_ref, f32[256,256]{1,0:T(8,128)S(1)} %get-tuple-element.19.spread_ref, f32[32,16,128]{2,1,0:T(8,128)S(1)} %get-tuple-element.20.taken_ref, ...), custom_call_target="tpu_custom_call" | custom-call | tf_op jit(solution)/shard_map/finish/pallas_call | solution.py:652
where the time goes:
time: 47.9 us; the launch traced here: 47.8 us
  Pallas kernels  46.5 us (97%)
  between operations  1.3 us (3%)
    pallas_call x1, Pallas kernels, on_device(): pl.pallas_call(functools.partial(collect_kernel, count, spaces), out_shap...  19.6 us
    pallas_call x1, Pallas kernels, on_device(): pl.pallas_call(functools.partial(regroup_kernel, count), out_shape=(squar...  17.9 us
    pallas_call x1, Pallas kernels, on_device(): pl.pallas_call(chain_kernel, out_shape=(square, square), in_specs=[smem,...  6.58 us
    pallas_call x1, Pallas kernels, on_device(): pl.pallas_call(finish_kernel, out_shape=(jax.ShapeDtypeStruct((1, 1, widt...  2.38 us

commit v1 on v0

--- a/solution.py
+++ b/solution.py
@@ -207,6 +207,63 @@
             pl.semaphore_signal(
                 barrier, inc=1, device_id={"energy": peer_of(me, step * stride)}, device_id_type=MESH)
     pl.semaphore_signal(barrier, inc=1, device_id={"energy": other}, device_id_type=MESH)
+
+    pl.semaphore_wait(barrier, 9)
+    own_half = pl.ds(pl.multiple_of(core * half, half), half)
+    other_half = pl.ds(pl.multiple_of((1 - core) * half, half), half)
+    given = (diag_ref, coup_ref)
+    stores = (diags_ref, coups_ref)
+
+    own_quarter = pl.ds(pl.multiple_of(half + core * (half // 2), half // 2), half // 2)
+    other_quarter = pl.ds(pl.multiple_of(half + (1 - core) * (half // 2), half // 2), half // 2)
+
+    class Pieces:
+        def __init__(self, kind, source, store, part, quarter, sems, device):
+            views = ((part,),) if kind else ((part, part), (quarter, pl.ds(0, half)))
+            self.copies = [
+                pltpu.make_async_remote_copy(
+                    src_ref=source.at[view], dst_ref=store.at[view], send_sem=sems[0][at], recv_sem=sems[1][at],
+                    device_id=device, device_id_type=MESH)
+                for at, view in enumerate(views)
+            ]
+
+        def start(self):
+            for copy in self.copies:
+                copy.start()
+
+        def wait_send(self):
+            for copy in self.copies:
+                copy.wait_send()
+
+        def wait_recv(self):
+            for copy in self.copies:
+                copy.wait_recv()
+
+    def far(way, stage):
+        kind = (way, 1 - way, way)[stage]
+        block = place if stage < 2 else sides[1 - way]
+        store = stores[kind].at[block]
+        source = given[kind].at[0] if stage < 2 else store
+        sems = (
+            (far_send.at[way, stage], more_sems.at[way, stage, 0]),
+            (far_recv.at[way, stage], more_sems.at[way, stage, 1]),
+        )
+        return Pieces(kind, source, store, own_half, own_quarter, sems, {"space": sides[way]})
+
+    def near(way, stage, own):
+        kind = (way, 1 - way, way)[stage]
+        block = sides[1 - way] if stage < 2 else across
+        store = stores[kind].at[block]
+        sems = (
+            (near_send.at[way, stage], more_sems.at[way, stage, 2]),
+            (near_recv.at[way, stage], more_sems.at[way, stage, 3]),
+        )
+        part, quarter = (own_half, own_quarter) if own else (other_half, other_quarter)
+        return Pieces(kind, store, store, part, quarter, sems, {"energy": other})
+
+    for stage in range(2):
+        for way in range(2):
+            far(way, stage).start()
 
     own_copies[0].wait()
     own_copies[1].wait()
@@ -229,63 +286,6 @@
         slots_ref[part, :, :size] = jnp.where(lower, jnp.where(pivot, 128, high - 128), low)
     own_bare[:, tail:] = jnp.zeros((1, 128), F32)
     own_bare[:, :span] = bare_in[...]
-
-    pl.semaphore_wait(barrier, 9)
-    own_half = pl.ds(pl.multiple_of(core * half, half), half)
-    other_half = pl.ds(pl.multiple_of((1 - core) * half, half), half)
-    given = (diag_ref, coup_ref)
-    stores = (diags_ref, coups_ref)
-
-    own_quarter = pl.ds(pl.multiple_of(half + core * (half // 2), half // 2), half // 2)
-    other_quarter = pl.ds(pl.multiple_of(half + (1 - core) * (half // 2), half // 2), half // 2)
-
-    class Pieces:
-        def __init__(self, kind, source, store, part, quarter, sems, device):
-            views = ((part,),) if kind else ((part, part), (quarter, pl.ds(0, half)))
-            self.copies = [
-                pltpu.make_async_remote_copy(
-                    src_ref=source.at[view], dst_ref=store.at[view], send_sem=sems[0][at], recv_sem=sems[1][at],
-                    device_id=device, device_id_type=MESH)
-                for at, view in enumerate(views)
-            ]
-
-        def start(self):
-            for copy in self.copies:
-                copy.start()
-
-        def wait_send(self):
-            for copy in self.copies:
-                copy.wait_send()
-
-        def wait_recv(self):
-            for copy in self.copies:
-                copy.wait_recv()
-
-    def far(way, stage):
-        kind = (way, 1 - way, way)[stage]
-        block = place if stage < 2 else sides[1 - way]
-        store = stores[kind].at[block]
-        source = given[kind].at[0] if stage < 2 else store
-        sems = (
-            (far_send.at[way, stage], more_sems.at[way, stage, 0]),
-            (far_recv.at[way, stage], more_sems.at[way, stage, 1]),
-        )
-        return Pieces(kind, source, store, own_half, own_quarter, sems, {"space": sides[way]})
-
-    def near(way, stage, own):
-        kind = (way, 1 - way, way)[stage]
-        block = sides[1 - way] if stage < 2 else across
-        store = stores[kind].at[block]
-        sems = (
-            (near_send.at[way, stage], more_sems.at[way, stage, 2]),
-            (near_recv.at[way, stage], more_sems.at[way, stage, 3]),
-        )
-        part, quarter = (own_half, own_quarter) if own else (other_half, other_quarter)
-        return Pieces(kind, store, store, part, quarter, sems, {"energy": other})
-
-    for stage in range(2):
-        for way in range(2):
-            far(way, stage).start()
 
     mine = own_pattern[me]
     bare = own_bare[...]

time: 47.9 us -> 47.9 us (level)
  no operation moved by 1% of the time
where the time goes in v1:
time: 47.9 us; the launch traced here: 47.8 us
  Pallas kernels  46.5 us (97%)
  between operations  1.3 us (3%)
    pallas_call x1, Pallas kernels, on_device(): pl.pallas_call(functools.partial(collect_kernel, count, spaces), out_shap...  19.6 us
    pallas_call x1, Pallas kernels, on_device(): pl.pallas_call(functools.partial(regroup_kernel, count), out_shape=(squar...  17.9 us
    pallas_call x1, Pallas kernels, on_device(): pl.pallas_call(chain_kernel, out_shape=(square, square), in_specs=[smem,...  6.58 us
    pallas_call x1, Pallas kernels, on_device(): pl.pallas_call(finish_kernel, out_shape=(jax.ShapeDtypeStruct((1, 1, widt...  2.38 us

profile of v1, /device:TPU:1, one launch (start us, length us, event | category | flops | bytes accessed | tf_op | source)
XLA Modules:
  0.0 47.8 jit_solution(6954535504835135108)
XLA Ops:
  1.3 19.6 %collect.1 = (f32[4,256,256]{2,1,0:T(8,128)S(1)}, f32[4,256,256]{2,1,0:T(8,128)S(1)}, s32[32,1,1408]{2,1,0:T(1,128)S(1)}, s32[32,1,1408]{2,1,0:T(1,128)S(1)}, f3...) custom-call(f32[1,256,256]{2,1,0:T(8,128)} %diag_ref.1, f32[1,256,256]{2,1,0:T(8,128)} %coup_ref.1, s32[1,43264]{1,0:T(1,128)} %pattern_ref.1, ...), custom_call_target="tpu_custom_call" | custom-call | tf_op jit(solution)/shard_map/collect/pallas_call | solution.py:604
  20.8 6.6 %chain.1 = (f32[256,256]{1,0:T(8,128)S(1)}, f32[256,256]{1,0:T(8,128)S(1)}) custom-call(f32[1]{0:T(128)S(6)} %copy.7.shift_ref, f32[4,256,256]{2,1,0:T(8,128)S(1)} %get-tuple-element.12.diags_ref, f32[4,256,256]{2,1,0:T(8,128)S(1)} %get-tuple-element.13.coups_ref), custom_call_target="tpu_custom_call" | custom-call | tf_op jit(solution)/shard_map/chain/pallas_call | solution.py:629
  27.4 17.9 %regroup.1 = (f32[256,256]{1,0:T(8,128)S(1)}, f32[32,16,128]{2,1,0:T(8,128)S(1)}) custom-call(f32[256,256]{1,0:T(8,128)S(1)} %get-tuple-element.15.base_ref, s32[32,1,1408]{2,1,0:T(1,128)S(1)} %get-tuple-element.16.rows_ref, s32[32,1,1408]{2,1,0:T(1,128)S(1)} %get-tuple-element.17.slots_ref, f32[8,256]{1,0:T(8,128)S(1)} %get-tuple-element.18.bare_pos_ref), custom_call_target="tpu_custom_call" | custom-call | tf_op jit(solution)/shard_map/regroup/pallas_call | solution.py:639
  45.4 2.4 %finish.1 = (f32[1,1,256,256]{3,2,1,0:T(8,128)}, f32[32,1,1352]{2,1,0:T(1,128)}) custom-call(f32[256,256]{1,0:T(8,128)S(1)} %get-tuple-element.14.reduced_ref, f32[256,256]{1,0:T(8,128)S(1)} %get-tuple-element.15.base_ref, f32[256,256]{1,0:T(8,128)S(1)} %get-tuple-element.19.spread_ref, f32[32,16,128]{2,1,0:T(8,128)S(1)} %get-tuple-element.20.taken_ref, ...), custom_call_target="tpu_custom_call" | custom-call | tf_op jit(solution)/shard_map/finish/pallas_call | solution.py:652

commit v2 on v0

--- a/solution.py
+++ b/solution.py
@@ -546,8 +546,10 @@
             for n in range(1, e + 1):
                 total = total + samples[e - n] * screened[n]
             selfen[e, :, cols] = total * (sigma_coef / count)
-    for peer in others:
-        to_peer(peer, selfen.at[peer], rows_of(spread_ref, me), sems_b).start()
+        for peer in others:
+            to_peer(
+                peer, selfen.at[peer, :, cols],
+                spread_ref.at[pl.ds(pl.multiple_of(me * 8, 8), 8), cols], sems_b).start()
     lax.fori_loop(PAIRS_FIRST + PAIRS_SECOND, pairs - 1, take_and_send, 0)
     take_pair(pairs - 1, 0)
     send_taken(peer_of(me, 1))

time: 47.9 us -> 48.1 us (level)
  no operation moved by 1% of the time
where the time goes in v2:
time: 48.1 us; the launch traced here: 48 us
  Pallas kernels  46.7 us (97%)
  between operations  1.3 us (3%)
    pallas_call x1, Pallas kernels, on_device(): pl.pallas_call(functools.partial(collect_kernel, count, spaces), out_shap...  19.6 us
    pallas_call x1, Pallas kernels, on_device(): pl.pallas_call(functools.partial(regroup_kernel, count), out_shape=(squar...  18.2 us
    pallas_call x1, Pallas kernels, on_device(): pl.pallas_call(chain_kernel, out_shape=(square, square), in_specs=[smem,...  6.58 us
    pallas_call x1, Pallas kernels, on_device(): pl.pallas_call(finish_kernel, out_shape=(jax.ShapeDtypeStruct((1, 1, widt...  2.37 us

profile of v2, /device:TPU:1, one launch (start us, length us, event | category | flops | bytes accessed | tf_op | source)
XLA Modules:
  0.0 48.0 jit_solution(8335107007750820253)
XLA Ops:
  1.3 19.6 %collect.1 = (f32[4,256,256]{2,1,0:T(8,128)S(1)}, f32[4,256,256]{2,1,0:T(8,128)S(1)}, s32[32,1,1408]{2,1,0:T(1,128)S(1)}, s32[32,1,1408]{2,1,0:T(1,128)S(1)}, f3...) custom-call(f32[1,256,256]{2,1,0:T(8,128)} %diag_ref.1, f32[1,256,256]{2,1,0:T(8,128)} %coup_ref.1, s32[1,43264]{1,0:T(1,128)} %pattern_ref.1, ...), custom_call_target="tpu_custom_call" | custom-call | tf_op jit(solution)/shard_map/collect/pallas_call | solution.py:606
  20.8 6.6 %chain.1 = (f32[256,256]{1,0:T(8,128)S(1)}, f32[256,256]{1,0:T(8,128)S(1)}) custom-call(f32[1]{0:T(128)S(6)} %copy.7.shift_ref, f32[4,256,256]{2,1,0:T(8,128)S(1)} %get-tuple-element.12.diags_ref, f32[4,256,256]{2,1,0:T(8,128)S(1)} %get-tuple-element.13.coups_ref), custom_call_target="tpu_custom_call" | custom-call | tf_op jit(solution)/shard_map/chain/pallas_call | solution.py:631
  27.4 18.2 %regroup.1 = (f32[256,256]{1,0:T(8,128)S(1)}, f32[32,16,128]{2,1,0:T(8,128)S(1)}) custom-call(f32[256,256]{1,0:T(8,128)S(1)} %get-tuple-element.15.base_ref, s32[32,1,1408]{2,1,0:T(1,128)S(1)} %get-tuple-element.16.rows_ref, s32[32,1,1408]{2,1,0:T(1,128)S(1)} %get-tuple-element.17.slots_ref, f32[8,256]{1,0:T(8,128)S(1)} %get-tuple-element.18.bare_pos_ref), custom_call_target="tpu_custom_call" | custom-call | tf_op jit(solution)/shard_map/regroup/pallas_call | solution.py:641
  45.6 2.4 %finish.1 = (f32[1,1,256,256]{3,2,1,0:T(8,128)}, f32[32,1,1352]{2,1,0:T(1,128)}) custom-call(f32[256,256]{1,0:T(8,128)S(1)} %get-tuple-element.14.reduced_ref, f32[256,256]{1,0:T(8,128)S(1)} %get-tuple-element.15.base_ref, f32[256,256]{1,0:T(8,128)S(1)} %get-tuple-element.19.spread_ref, f32[32,16,128]{2,1,0:T(8,128)S(1)} %get-tuple-element.20.taken_ref, ...), custom_call_target="tpu_custom_call" | custom-call | tf_op jit(solution)/shard_map/finish/pallas_call | solution.py:654
